TPU v7x, 32 devices: a whole 2x2x4 slice. The times are simulated.
32 devices in a mesh: dp: 16 (over z, y, core), seq: 2 (over x).
Axes of the slice: x: 2, y: 2, z: 4, core: 2. Of those that a mesh axis runs over, the one named last changes fastest.
Arguments:
- latents: bfloat16 [2, 16, 1024, 1152], P(None, 'dp', 'seq'), may hold values from -6 to 6
- cond: float32 [24, 1152], replicated, may hold values from -6 to 6
- slot_mask: int32 [2, 16], replicated, may hold values from 0 to 1, as said below
- slot_image: int32 [2, 16], replicated, may hold values from 0 to 23, as said below
- teacher: bfloat16 [2, 16, 1024, 1152], P(None, 'dp', 'seq'), may hold values from -6 to 6
- cotangent: bfloat16 [2, 16, 1024, 1152], P(None, 'dp', 'seq'), may hold values from -6 to 6
- ada_w: bfloat16 [1152, 6912], P('dp', 'seq'), may hold values from -0.1875 to 0.1875
- ada_b: float32 [6912], replicated, may hold values from -3 to 3
- qkv_w: bfloat16 [1152, 3456], P('dp', 'seq'), may hold values from -0.1875 to 0.1875
- qv_b: float32 [2304], replicated, may hold values from -2 to 2
- proj_w: bfloat16 [1152, 1152], P('dp', 'seq'), may hold values from -1.5 to 1.5
- proj_b: float32 [1152], replicated, may hold values from -2 to 2
- fc1_w: bfloat16 [1152, 4608], P('dp', 'seq'), may hold values from -0.1875 to 0.1875
- fc1_b: float32 [4608], replicated, may hold values from -2 to 2
- fc2_w: bfloat16 [4608, 1152], P('dp', 'seq'), may hold values from -0.09375 to 0.09375
- fc2_b: float32 [1152], replicated, may hold values from -2 to 2
Outputs:
- block_out: bfloat16 [2, 16, 1024, 1152], P(None, 'dp', 'seq')
- latents_grad: float32 [2, 16, 1024, 1152], P(None, 'dp', 'seq')
- loss: float32 [], replicated
- cond_grad: float32 [24, 1152], replicated
- ada_w_grad: float32 [1152, 6912], P('dp', 'seq')
- ada_b_grad: float32 [6912], replicated
- qkv_w_grad: float32 [1152, 3456], P('dp', 'seq')
- qv_b_grad: float32 [2304], replicated
- proj_w_grad: float32 [1152, 1152], P('dp', 'seq')
- proj_b_grad: float32 [1152], replicated
- fc1_w_grad: float32 [1152, 4608], P('dp', 'seq')
- fc1_b_grad: float32 [4608], replicated
- fc2_w_grad: float32 [4608, 1152], P('dp', 'seq')
- fc2_b_grad: float32 [1152], replicated
Inputs may be any that keep to these rules, and one draw needn't show every extreme that they name: Micro-batch i holds the images n with n mod 2 = i, each in exactly one slot with slot_mask 1; all other slots have slot_mask 0. `slot_image`: in a slot with slot_mask 1, the image it holds; in a pad slot any image number.
All inputs are finite; a program needn't handle non-finite values.
Results may differ from a plain program's by a relative error of at most 0.018.
The roundings to bfloat16 on the way count: a program that leaves them out, or rounds other values in their place, can miss the bound.
Values may be sent and summed in bfloat16 or wider, within the bound.
A program may use at most 448 MiB of HBM per device.

v0:
```python
import jax
import jax.numpy as jnp
from jax import lax
from jax.sharding import PartitionSpec as P

HEADS = 16


HIGH = lax.Precision.HIGHEST


def layer_norm(value):
    center = value - jnp.mean(value, axis=-1, keepdims=True)
    spread = jnp.mean(center * center, axis=-1, keepdims=True)
    return center * lax.rsqrt(spread + 1e-06)


def gelu_tanh(value):
    return jax.nn.gelu(value, approximate=True)


def local(
    latents,
    cond,
    slot_mask,
    slot_image,
    teacher,
    cotangent,
    ada_w,
    ada_b,
    qkv_w,
    qv_b,
    proj_w,
    proj_b,
    fc1_w,
    fc1_b,
    fc2_w,
    fc2_b,
):
    f32 = jnp.float32
    bf16 = jnp.bfloat16
    micro = latents.shape[0]
    slots_dev = latents.shape[1]
    local_len = latents.shape[2]
    width = latents.shape[3]
    images = cond.shape[0]
    heads = HEADS
    head_size = width // heads
    full_len = local_len * lax.axis_size("seq")
    hidden_units = fc1_b.shape[0]
    scale = head_size ** (-0.5)
    dp_index = lax.axis_index("dp")
    seq_index = lax.axis_index("seq")
    mod_cols = ada_w.shape[1]
    col_start = seq_index * mod_cols
    count = jnp.sum(slot_mask).astype(f32) * full_len
    divisor = count * width
    image_table = jnp.arange(images, dtype=jnp.int32)
    grad_qkv = jnp.zeros((width, 3 * width), f32)
    grad_proj = jnp.zeros((width, width), f32)
    grad_fc1 = jnp.zeros((width, hidden_units), f32)
    grad_fc2 = jnp.zeros((hidden_units, width), f32)
    grad_ada = jnp.zeros((width, mod_cols), f32)
    grad_cond = jnp.zeros((images, width), f32)
    bias_ada = jnp.zeros((6 * width,), f32)
    bias_qv = jnp.zeros((2 * width,), f32)
    bias_proj = jnp.zeros((width,), f32)
    bias_fc1 = jnp.zeros((hidden_units,), f32)
    bias_fc2 = jnp.zeros((width,), f32)
    loss_sum = jnp.zeros((), f32)
    column_ids = jnp.arange(6 * width, dtype=jnp.int32)
    in_mine = (column_ids >= col_start) & (column_ids < col_start + mod_cols)
    results = []
    input_grads = []
    for micro_index in range(micro):
        qkv_cols = lax.all_gather(qkv_w, "seq", axis=1, tiled=True)
        proj_cols = lax.all_gather(proj_w, "seq", axis=1, tiled=True)
        fc1_cols = lax.all_gather(fc1_w, "seq", axis=1, tiled=True)
        fc2_cols = lax.all_gather(fc2_w, "seq", axis=1, tiled=True)
        qkv_full = lax.all_gather(qkv_cols, "dp", axis=0, tiled=True)
        proj_full = lax.all_gather(proj_cols, "dp", axis=0, tiled=True)
        fc1_full = lax.all_gather(fc1_cols, "dp", axis=0, tiled=True)
        fc2_full = lax.all_gather(fc2_cols, "dp", axis=0, tiled=True)
        ada_cols = lax.all_gather(ada_w, "seq", axis=1, tiled=True)
        ada_full = lax.all_gather(ada_cols, "dp", axis=0, tiled=True)
        qkv_full, proj_full, fc1_full, fc2_full, ada_full = (
            qkv_full,
            proj_full,
            fc1_full,
            fc2_full,
            ada_full,
        )
        image_mine = lax.dynamic_slice_in_dim(
            slot_image[micro_index], dp_index * slots_dev, slots_dev
        )
        mask_mine = lax.dynamic_slice_in_dim(
            slot_mask[micro_index], dp_index * slots_dev, slots_dev
        ).astype(f32)
        pick_mine = (image_mine[:, None] == image_table[None, :]).astype(f32)
        cond_mine = jnp.dot(pick_mine, cond, precision=HIGH)
        silu_mine = jax.nn.silu(cond_mine).astype(bf16)
        modulation = jnp.dot(silu_mine, ada_full, preferred_element_type=f32) + ada_b
        pieces = [
            modulation[:, index * width : (index + 1) * width][:, None, :] for index in range(6)
        ]
        shift1, scale1, gate1, shift2, scale2, gate2 = pieces
        inputs = latents[micro_index].astype(f32)
        normed1 = layer_norm(inputs)
        hidden = (normed1 * (1.0 + scale1) + shift1).astype(bf16)
        joint = jnp.einsum("btd,de->bte", hidden, qkv_full, preferred_element_type=f32)
        query = (joint[..., :width] + qv_b[:width]).astype(bf16)
        keys_local = joint[..., width : 2 * width].astype(bf16)
        values_local = (joint[..., 2 * width :] + qv_b[width:]).astype(bf16)
        keys_all, values_all = (
            lax.all_gather(keys_local, "seq", axis=1, tiled=True),
            lax.all_gather(values_local, "seq", axis=1, tiled=True),
        )
        query_heads = query.reshape(slots_dev, local_len, heads, head_size)
        key_heads = keys_all.reshape(slots_dev, full_len, heads, head_size)
        value_heads = values_all.reshape(slots_dev, full_len, heads, head_size)
        scores = (
            jnp.einsum("bqhe,bkhe->bhqk", query_heads, key_heads, preferred_element_type=f32)
            * scale
        )
        row_top = jnp.max(scores, axis=-1, keepdims=True)
        row_total = jnp.sum(jnp.exp(scores - row_top), axis=-1, keepdims=True)
        probs_low = (jnp.exp(scores - row_top) / row_total).astype(bf16)
        attended = jnp.einsum("bhqk,bkhe->bqhe", probs_low, value_heads, preferred_element_type=f32)
        attended = attended.reshape(slots_dev, local_len, width).astype(bf16)
        branch = jnp.einsum("btd,de->bte", attended, proj_full, preferred_element_type=f32) + proj_b
        middle = inputs + gate1 * branch
        normed2 = layer_norm(middle)
        hidden2 = (normed2 * (1.0 + scale2) + shift2).astype(bf16)
        before = jnp.einsum("btd,df->btf", hidden2, fc1_full, preferred_element_type=f32) + fc1_b
        active = gelu_tanh(before).astype(bf16)
        mlp_out = jnp.einsum("btf,fd->btd", active, fc2_full, preferred_element_type=f32) + fc2_b
        result = middle + gate2 * mlp_out
        results.append(result.astype(bf16))
        valid = mask_mine[:, None, None]
        diff = result - teacher[micro_index].astype(f32)
        loss_sum = loss_sum + jnp.sum(valid * diff * diff)
        grad_out = valid * (2.0 * diff / divisor + cotangent[micro_index].astype(f32))
        d_gate2 = jnp.sum(grad_out * mlp_out, axis=1)
        d_mlp = (grad_out * gate2).astype(bf16)
        grad_fc2 = grad_fc2 + jnp.einsum("btf,btd->fd", active, d_mlp, preferred_element_type=f32)
        bias_fc2 = bias_fc2 + jnp.sum(d_mlp.astype(f32), axis=(0, 1))
        d_active = jnp.einsum("btd,fd->btf", d_mlp, fc2_full, preferred_element_type=f32)
        d_before = jax.vjp(gelu_tanh, before)[1](d_active)[0].astype(bf16)
        grad_fc1 = grad_fc1 + jnp.einsum(
            "btd,btf->df", hidden2, d_before, preferred_element_type=f32
        )
        bias_fc1 = bias_fc1 + jnp.sum(d_before.astype(f32), axis=(0, 1))
        d_hidden2 = jnp.einsum("btf,df->btd", d_before, fc1_full, preferred_element_type=f32)
        d_scale2 = jnp.sum(d_hidden2 * normed2, axis=1)
        d_shift2 = jnp.sum(d_hidden2, axis=1)
        d_middle = grad_out + jax.vjp(layer_norm, middle)[1](d_hidden2 * (1.0 + scale2))[0]
        d_gate1 = jnp.sum(d_middle * branch, axis=1)
        d_branch = (d_middle * gate1).astype(bf16)
        grad_proj = grad_proj + jnp.einsum(
            "btd,bte->de", attended, d_branch, preferred_element_type=f32
        )
        bias_proj = bias_proj + jnp.sum(d_branch.astype(f32), axis=(0, 1))
        d_attended = jnp.einsum(
            "bte,de->btd", d_branch, proj_full, preferred_element_type=f32
        ).astype(bf16)
        d_attended = d_attended.reshape(slots_dev, local_len, heads, head_size)
        again_scores = (
            jnp.einsum("bqhe,bkhe->bhqk", query_heads, key_heads, preferred_element_type=f32)
            * scale
        )
        probs = jnp.exp(again_scores - row_top) / row_total
        d_probs = jnp.einsum("bqhe,bkhe->bhqk", d_attended, value_heads, preferred_element_type=f32)
        row_inner = jnp.sum(probs * d_probs, axis=-1, keepdims=True)
        d_scores = (probs * (d_probs - row_inner)).astype(bf16)
        d_query = (
            jnp.einsum("bhqk,bkhe->bqhe", d_scores, key_heads, preferred_element_type=f32) * scale
        )
        key_terms = (
            jnp.einsum("bhqk,bqhe->bkhe", d_scores, query_heads, preferred_element_type=f32) * scale
        )
        value_terms = jnp.einsum(
            "bhqk,bqhe->bkhe", probs_low, d_attended, preferred_element_type=f32
        )
        key_terms = key_terms.reshape(slots_dev, full_len, width)
        value_terms = value_terms.reshape(slots_dev, full_len, width)
        d_keys, d_values = (
            lax.psum_scatter(
                key_terms.astype(jnp.bfloat16), "seq", scatter_dimension=1, tiled=True
            ).astype(jnp.float32),
            lax.psum_scatter(
                value_terms.astype(jnp.bfloat16), "seq", scatter_dimension=1, tiled=True
            ).astype(jnp.float32),
        )
        d_query = d_query.reshape(slots_dev, local_len, width).astype(bf16)
        d_joint = jnp.concatenate([d_query, d_keys.astype(bf16), d_values.astype(bf16)], axis=-1)
        grad_qkv = grad_qkv + jnp.einsum("btd,bte->de", hidden, d_joint, preferred_element_type=f32)
        bias_qv = bias_qv + jnp.concatenate(
            [
                jnp.sum(d_joint[..., :width].astype(f32), axis=(0, 1)),
                jnp.sum(d_joint[..., 2 * width :].astype(f32), axis=(0, 1)),
            ]
        )
        d_hidden = jnp.einsum("bte,de->btd", d_joint, qkv_full, preferred_element_type=f32)
        d_scale1 = jnp.sum(d_hidden * normed1, axis=1)
        d_shift1 = jnp.sum(d_hidden, axis=1)
        d_inputs = d_middle + jax.vjp(layer_norm, inputs)[1](d_hidden * (1.0 + scale1))[0]
        input_grads.append(d_inputs)
        mod_partial = jnp.concatenate(
            [d_shift1, d_scale1, d_gate1, d_shift2, d_scale2, d_gate2], axis=-1
        )
        d_mod = lax.psum(mod_partial, "seq").astype(bf16)
        own_cols = lax.dynamic_slice_in_dim(d_mod, col_start, mod_cols, 1)
        bias_ada = bias_ada + jnp.where(in_mine, jnp.sum(d_mod.astype(f32), axis=0), 0.0)
        grad_ada = grad_ada + jnp.dot(silu_mine.T, own_cols, preferred_element_type=f32)
        ada_own = lax.dynamic_slice_in_dim(ada_full, col_start, mod_cols, 1)
        d_cond = jnp.einsum("bm,dm->bd", own_cols, ada_own, preferred_element_type=f32)
        d_cond = jax.vjp(jax.nn.silu, cond_mine)[1](d_cond)[0]
        grad_cond = grad_cond + jnp.dot(pick_mine.T, d_cond, precision=HIGH)
    ada_w_grad = lax.psum_scatter(
        grad_ada.astype(jnp.bfloat16), "dp", scatter_dimension=0, tiled=True
    ).astype(jnp.float32)
    rows_qkv, rows_proj, rows_fc1, rows_fc2 = (
        lax.psum_scatter(
            grad_qkv.astype(jnp.bfloat16), "dp", scatter_dimension=0, tiled=True
        ).astype(jnp.float32),
        lax.psum_scatter(
            grad_proj.astype(jnp.bfloat16), "dp", scatter_dimension=0, tiled=True
        ).astype(jnp.float32),
        lax.psum_scatter(
            grad_fc1.astype(jnp.bfloat16), "dp", scatter_dimension=0, tiled=True
        ).astype(jnp.float32),
        lax.psum_scatter(
            grad_fc2.astype(jnp.bfloat16), "dp", scatter_dimension=0, tiled=True
        ).astype(jnp.float32),
    )
    qkv_w_grad, proj_w_grad, fc1_w_grad, fc2_w_grad = (
        lax.psum_scatter(
            rows_qkv.astype(jnp.bfloat16), "seq", scatter_dimension=1, tiled=True
        ).astype(jnp.float32),
        lax.psum_scatter(
            rows_proj.astype(jnp.bfloat16), "seq", scatter_dimension=1, tiled=True
        ).astype(jnp.float32),
        lax.psum_scatter(
            rows_fc1.astype(jnp.bfloat16), "seq", scatter_dimension=1, tiled=True
        ).astype(jnp.float32),
        lax.psum_scatter(
            rows_fc2.astype(jnp.bfloat16), "seq", scatter_dimension=1, tiled=True
        ).astype(jnp.float32),
    )
    summed = lax.psum(
        (loss_sum, bias_ada, bias_qv, bias_proj, bias_fc1, bias_fc2, grad_cond), ("dp", "seq")
    )
    loss = summed[0] / divisor
    block_out = jnp.stack(results, axis=0)
    latents_grad = jnp.stack(input_grads, axis=0)
    return (
        block_out,
        latents_grad,
        loss,
        summed[6],
        ada_w_grad,
        summed[1],
        qkv_w_grad,
        summed[2],
        proj_w_grad,
        summed[3],
        fc1_w_grad,
        summed[4],
        fc2_w_grad,
        summed[5],
    )


def solution(mesh):
    placed = (
        P(None, "dp", "seq", None),
        P(),
        P(),
        P(),
        P(None, "dp", "seq", None),
        P(None, "dp", "seq", None),
        P("dp", "seq"),
        P(),
        P("dp", "seq"),
        P(),
        P("dp", "seq"),
        P(),
        P("dp", "seq"),
        P(),
        P("dp", "seq"),
        P(),
    )
    return jax.shard_map(
        local,
        mesh=mesh,
        in_specs=placed,
        out_specs=(
            P(None, "dp", "seq", None),
            P(None, "dp", "seq", None),
            P(),
            P(),
            P("dp", "seq"),
            P(),
            P("dp", "seq"),
            P(),
            P("dp", "seq"),
            P(),
            P("dp", "seq"),
            P(),
            P("dp", "seq"),
            P(),
        ),
        check_vma=False,
    )
```

profile of v0, /device:TPU:0, one launch (start us, length us, event | category | flops | bytes accessed | tf_op | source)
XLA Modules:
  0.0 1624.1 jit_solution(10174713782407896748)
XLA Ops:
  7.3 18.1 %all_gather.52 = bf16[72,6912]{1,0:T(8,128)(2,1)} all-gather(bf16[72,3456]{1,0:T(8,128)(2,1)} %param.22), channel_id=1, replica_groups=mesh['dp'=16,'seq'=2] {'seq'}, dimensions={1}, use_global_device_ids=true | all-gather | bytes 1492992 | tf_op jit(solution)/shard_map/all_gather | solution.py:84
  41.8 105.5 %all-gather.13.cloned.1.call-done = bf16[1152,6912]{1,0:T(8,128)(2,1)} async-done(((bf16[72,6912]{1,0:T(8,128)(2,1)}), bf16[1152,6912]{1,0:T(8,128)(2,1)}) %all-gather.13.cloned.1.call-update) | async-done | bytes 15925264 | tf_op jit(solution)/shard_map/all_gather | solution.py:85
  160.7 59.7 %all-gather.15.cloned.1.call-done = bf16[1152,3456]{1,0:T(8,128)(2,1)} async-done(((bf16[72,3456]{1,0:T(8,128)(2,1)}), bf16[1152,3456]{1,0:T(8,128)(2,1)}) %all-gather.15.cloned.1.call-update) | async-done | bytes 7962640 | tf_op jit(solution)/shard_map/all_gather | solution.py:80
  258.1 17.7 %all_gather.60 = bf16[72,4608]{1,0:T(8,128)(2,1)} all-gather(bf16[72,2304]{1,0:T(8,128)(2,1)S(1)} %copy-done.31), channel_id=1, replica_groups=mesh['dp'=16,'seq'=2] {'seq'}, dimensions={1}, use_global_device_ids=true | all-gather | bytes 995328 | tf_op jit(solution)/shard_map/all_gather | solution.py:78
  275.9 10.2 all-gather.2
  299.1 15.0 all-gather.27.cloned.1.call-done
  318.4 33.2 %all-gather.17.cloned.1.call-done = bf16[1,1024,1152]{2,1,0:T(8,128)(2,1)} async-done(((bf16[1,512,1152]{2,1,0:T(8,128)(2,1)}), bf16[1,1024,1152]{2,1,0:T(8,128)(2,1)}) %all-gather.17.cloned.1.call-update) | async-done | bytes 2359312 | tf_op jit(solution)/shard_map/all_gather | solution.py:116
  355.8 33.2 %all-gather.19.cloned.1.call-done = bf16[1,1024,1152]{2,1,0:T(8,128)(2,1)} async-done(((bf16[1,512,1152]{2,1,0:T(8,128)(2,1)}), bf16[1,1024,1152]{2,1,0:T(8,128)(2,1)}) %all-gather.19.cloned.1.call-update) | async-done | bytes 2359312 | tf_op jit(solution)/shard_map/all_gather | solution.py:115
  393.4 17.4 %fusion.192 = (f32[16,512]{1,0:T(8,128)S(1)}, f32[16,512,1024]{2,1,0:T(8,128)}) fusion(bf16[512,16,72]{0,2,1:T(8,128)(2,1)} %bitcast.285, bf16[1024,16,72]{0,2,1:T(8,128)(2,1)} %bitcast.281), kind=kOutput, calls=%fused_computation.324 | convolution fusion | flops 1233126400 | bytes 37126144 | tf_op jit(solution)/shard_map/sub | solution.py:127
  410.8 15.5 fusion.97
  440.6 17.9 %fusion.191 = (f32[16,512]{1,0:T(8,128)S(1)}, f32[16,512,1024]{2,1,0:T(8,128)}) fusion(bf16[512,16,72]{0,2,1:T(8,128)(2,1)} %bitcast.287, bf16[1024,16,72]{0,2,1:T(8,128)(2,1)} %bitcast.283), kind=kOutput, calls=%fused_computation.323 | convolution fusion | flops 1233126400 | bytes 37126144 | tf_op jit(solution)/shard_map/sub | solution.py:127
  458.5 15.2 fusion.94
  483.9 41.0 %all-gather.23.cloned.1.call-done = bf16[1152,4608]{1,0:T(8,128)(2,1)} async-done(((bf16[72,4608]{1,0:T(8,128)(2,1)}), bf16[1152,4608]{1,0:T(8,128)(2,1)}) %all-gather.23.cloned.1.call-update) | async-done | bytes 10616848 | tf_op jit(solution)/shard_map/all_gather | solution.py:82
  524.9 12.5 fusion.171
  546.5 68.1 %all-gather.25.cloned.1.call-done = bf16[4608,1152]{1,0:T(8,128)(2,1)} async-done(((bf16[288,1152]{1,0:T(8,128)(2,1)}), bf16[4608,1152]{1,0:T(8,128)(2,1)}) %all-gather.25.cloned.1.call-update) | async-done | bytes 10616848 | tf_op jit(solution)/shard_map/all_gather | solution.py:83
  614.7 13.9 convolution_add_fusion.4
  628.5 20.5 %convert_reduce_fusion.5 = (f32[1152]{0:T(1024)}, bf16[512,1152]{1,0:T(8,128)(2,1)}, f32[512,1152]{1,0:T(8,128)}, f32[512,1152]{1,0:T(8,128)}, f32[1152]{0:T(102...) fusion(f32[1152]{0:T(1024)S(1)} %copy-done.92, ...), kind=kOutput, calls=%fused_computation.144 | convolution fusion | flops 5475334144 | bytes 46047756 | tf_op jit(solution)/shard_map/btf,fd->btd/dot_general | solution.py:136
  649.1 13.3 fusion.194
  662.4 25.8 %convert_reduce_fusion.1 = (f32[4608]{0:T(1024)}, bf16[512,4608]{1,0:T(8,128)(2,1)}, f32[4608]{0:T(1024)}, bf16[512,4608]{1,0:T(8,128)(2,1)S(1)}) fusion(f32[512,4608]{1,0:T(8,128)} %fusion.171, f32[4608]{0:T(1024)S(1)} %copy-done.100, f32[512,4608]{1,0:T(8,128)} %fusion.194, f32[512,4608]{1,0:T(8,128)} %fusion.172, bf16[512,1152]{1,0:T(8,128)(2,1)S(1)} %copy-done.106, ...), kind=kOutput, calls=%fused_computation.43 | convolution fusion | flops 5544336384 | bytes 49600512 | tf_op jit(solution)/shard_map/btd,fd->btf/dot_general | solution.py:147
  688.2 14.3 multiply_reduce_fusion.5
  702.5 12.4 multiply_reduce_fusion.8
  745.0 23.4 %multiply_reduce_fusion.1 = (f32[16,512]{1,0:T(8,128)S(1)}, f32[16,512,1024]{2,1,0:T(8,128)}) fusion(f32[16,512,1024]{2,1,0:T(8,128)} %get-tuple-element.114, f32[16,512]{1,0:T(8,128)S(1)} %copy-done.46, bf16[512,16,72]{0,2,1:T(8,128)(2,1)} %bitcast.312, bf16[1024,16,72]{0,2,1:T(8,128)(2,1)} %bitcast.301), kind=kOutput, calls=%fused_computation.5 | convolution fusion | flops 1233117184 | bytes 70713344 | tf_op jit(solution)/shard_map/bqhe,bkhe->bhqk/dot_general | solution.py:172
  773.8 14.1 fusion.88
  788.0 28.3 %multiply_convert_fusion.1 = bf16[16,512,1024]{2,1,0:T(8,128)(2,1)} fusion(f32[16,512,1024]{2,1,0:T(8,128)} %get-tuple-element.121, f32[16,512]{1,0:T(8,128)S(1)} %get-tuple-element.120, f32[16,512,1024]{2,1,0:T(8,128)} %get-tuple-element.114, f32[16,512]{1,0:T(8,128)S(1)} %copy-done.46), kind=kLoop, calls=%fused_computation.4 | loop fusion | flops 33554432 | bytes 83951616 | tf_op jit(solution)/shard_map/convert_element_type | solution.py:174
  816.2 10.4 multiply_convert_fusion.5
  827.4 14.6 fusion.91
  842.0 22.9 %multiply_reduce_fusion = (f32[16,512]{1,0:T(8,128)S(1)}, f32[16,512,1024]{2,1,0:T(8,128)}) fusion(f32[16,512,1024]{2,1,0:T(8,128)} %get-tuple-element.116, f32[16,512]{1,0:T(8,128)S(1)} %copy-done.44, bf16[512,16,72]{0,2,1:T(8,128)(2,1)} %bitcast.311, bf16[1024,16,72]{0,2,1:T(8,128)(2,1)S(1)} %bitcast.299), kind=kOutput, calls=%fused_computation.3 | convolution fusion | flops 1233117184 | bytes 70713344 | tf_op jit(solution)/shard_map/bqhe,bkhe->bhqk/dot_general | solution.py:172
  864.9 28.7 %multiply_convert_fusion = bf16[16,512,1024]{2,1,0:T(8,128)(2,1)} fusion(f32[16,512,1024]{2,1,0:T(8,128)} %get-tuple-element.126, f32[16,512]{1,0:T(8,128)S(1)} %get-tuple-element.125, f32[16,512,1024]{2,1,0:T(8,128)} %get-tuple-element.116, f32[16,512]{1,0:T(8,128)S(1)} %copy-done.44), kind=kLoop, calls=%fused_computation.2 | loop fusion | flops 33554432 | bytes 83951616 | tf_op jit(solution)/shard_map/convert_element_type | solution.py:174
  893.6 10.4 multiply_convert_fusion.4
  905.3 14.7 fusion.173
  920.0 17.1 %fusion.9 = bf16[4608,1152]{1,0:T(8,128)(2,1)} fusion(f32[4608,1152]{1,0:T(8,128)} %fusion.173, bf16[512,1152]{1,0:T(8,128)(2,1)S(1)} %copy-done.105, f32[512,4608]{1,0:T(8,128)} %fusion.172, f32[4608]{0:T(1024)S(1)} %copy-done.101), kind=kOutput, calls=%fused_computation.15 | convolution fusion | flops 5470027776 | bytes 42485760 | tf_op jit(solution)/shard_map/btf,btd->fd/dot_general | solution.py:145
  937.8 12.9 fusion.170
  950.7 16.3 %fusion.8 = bf16[1152,4608]{1,0:T(8,128)(2,1)} fusion(f32[1152,4608]{1,0:T(8,128)} %fusion.170, bf16[512,4608]{1,0:T(8,128)(2,1)} %copy-done.103, f32[512,1152]{1,0:T(8,128)S(1)} %copy-done.8, f32[1152]{0:T(1024)S(1)} %copy-done.88, f32[1152]{0:T(1024)S(1)} %copy-done.51, f32[512]{0:T(512)S(1)} %copy-done.78, f32[512]{0:T(512)S(1)} %copy-done.66), kind=kOutput, calls=%fused_computation.14 | convolution fusion | flops 5449383936 | bytes 38941696 | tf_op jit(solution)/shard_map/btd,btf->df/dot_general | solution.py:149
  968.9 14.1 convert_reduce_fusion.11
  983.0 12.9 convert_reduce_fusion.9
  998.1 12.4 fusion.101
  1010.6 14.8 fusion.12
  1025.9 9.5 fusion.65
  1035.5 10.6 fusion.60
  1051.8 15.7 all-reduce.4
  1081.0 122.0 %reduce-scatter.34.cloned.1.call-done = bf16[72,4608]{1,0:T(8,128)(2,1)} async-done(((bf16[1152,4608]{1,0:T(8,128)(2,1)}), bf16[72,4608]{1,0:T(8,128)(2,1)}) %reduce-scatter.34.cloned.1.call-update) | async-done | bytes 663568 | tf_op jit(solution)/shard_map/reduce_scatter | solution.py:229
  1224.9 98.0 %reduce-scatter.48.cloned.1.call-done = bf16[72,3456]{1,0:T(8,128)(2,1)} async-done(((bf16[1152,3456]{1,0:T(8,128)(2,1)}), bf16[72,3456]{1,0:T(8,128)(2,1)}) %reduce-scatter.48.cloned.1.call-update) | async-done | bytes 497680
  1339.7 44.9 %all-reduce.3 = (f32[]{:T(128)}, f32[6912]{0:T(1024)}, f32[2304]{0:T(1024)}, f32[1152]{0:T(1024)}, f32[4608]{0:T(1024)}, /*index=5*/f32[1152]{0:T(1024)}) all-reduce(f32[]{:T(128)S(6)} %add.469, f32[6912]{0:T(1024)S(1)} %select_add_fusion, f32[2304]{0:T(1024)S(1)} %maximum_add_fusion, ...), channel_id=1, replica_groups=mesh['dp'=16,'seq'=2] {'dp','seq'}, use_global_device_ids=true, to_apply=%region_29.30 | all-reduce | flops 16129 | bytes 129032 | tf_op jit(solution)/shard_map/psum | solution.py:250
  1385.3 42.8 %reduce-scatter.46.cloned.1.call-done = bf16[72,3456]{1,0:T(8,128)(2,1)} async-done(((bf16[1152,3456]{1,0:T(8,128)(2,1)}), bf16[72,3456]{1,0:T(8,128)(2,1)}) %reduce-scatter.46.cloned.1.call-update) | async-done | bytes 497680
  1430.2 18.5 %reduce-scatter.44.cloned.1.call-done = bf16[576,288]{1,0:T(8,128)(2,1)} async-done(((bf16[1152,288]{1,0:T(8,128)(2,1)}), bf16[576,288]{1,0:T(8,128)(2,1)}) %reduce-scatter.44.cloned.1.call-update) | async-done | bytes 331792
  1450.8 16.3 %reduce-scatter.36.cloned.1.call-done = bf16[72,2304]{1,0:T(8,128)(2,1)} async-done(((bf16[72,4608]{1,0:T(8,128)(2,1)}), bf16[72,2304]{1,0:T(8,128)(2,1)}) %reduce-scatter.36.cloned.1.call-update) | async-done | bytes 331792 | tf_op jit(solution)/shard_map/reduce_scatter | solution.py:243
  1469.0 19.0 %reduce-scatter.40.cloned.1.call-done = bf16[1728,72]{1,0:T(8,128)(2,1)} async-done(((bf16[3456,72]{1,0:T(8,128)(2,1)}), bf16[1728,72]{1,0:T(8,128)(2,1)}) %reduce-scatter.40.cloned.1.call-update) | async-done | bytes 248848
  1490.0 124.7 %all-reduce.7.cloned.1.call-done = f32[24,1152]{1,0:T(8,128)} async-done(((f32[24,1152]{1,0:T(8,128)}), f32[24,1152]{1,0:T(8,128)}) %all-reduce.7.cloned.1.call-update) | async-done | bytes 110608 | tf_op jit(solution)/shard_map/psum | solution.py:250
  (398 shorter events, 234.5 us)
Async XLA Ops:
  7.2 28.8 %copy-start = (f32[24,1152]{1,0:T(8,128)S(1)}, f32[24,1152]{1,0:T(8,128)}, u32[]{:S(2)}) copy-start(f32[24,1152]{1,0:T(8,128)} %param.17) | copy-start | bytes 331780
  7.2 140.1 %all-gather.13.cloned.1.call-start = ((), (), s32[]{:S(2)}) async-start(), calls=%async_computation.13 | async-start | bytes 16920576 | tf_op jit(solution)/shard_map/all_gather | solution.py:85
  25.3 195.2 %all-gather.15.cloned.1.call-start = ((), (), s32[]{:S(2)}) async-start(), calls=%async_computation.14 | async-start | bytes 8460288 | tf_op jit(solution)/shard_map/all_gather | solution.py:80
  35.2 259.6 %all-gather.29.cloned.1.call-start = ((), (), s32[]{:S(2)}) async-start(), calls=%async_computation.21 | async-start | bytes 3538944 | tf_op jit(solution)/shard_map/all_gather | solution.py:115
  40.5 180.0 %copy-start.41 = (f32[512]{0:T(512)}, f32[512]{0:T(512)S(1)}, u32[]{:S(2)}) copy-start(f32[512]{0:T(512)S(1)} %get-tuple-element.136) | copy-start | bytes 6148
  40.5 192.5 %copy-start.69 = (f32[512]{0:T(512)}, f32[512]{0:T(512)S(1)}, u32[]{:S(2)}) copy-start(f32[512]{0:T(512)S(1)} %get-tuple-element.137) | copy-start | bytes 6148
  41.8 191.2 %copy-start.75 = (f32[512]{0:T(512)}, f32[512]{0:T(512)S(1)}, u32[]{:S(2)}) copy-start(f32[512]{0:T(512)S(1)} %fusion.152) | copy-start | bytes 6148
  41.8 178.7 %copy-start.63 = (f32[512]{0:T(512)}, f32[512]{0:T(512)S(1)}, u32[]{:S(2)}) copy-start(f32[512]{0:T(512)S(1)} %fusion.154) | copy-start | bytes 6148
  160.7 67.5 %copy-start.35 = (f32[1152]{0:T(1024)}, f32[1152]{0:T(1024)S(1)}, u32[]{:S(2)}) copy-start(f32[1152]{0:T(1024)S(1)} %get-tuple-element.43) | copy-start | bytes 13828
  160.7 67.5 %copy-start.81 = (f32[1152]{0:T(1024)}, f32[1152]{0:T(1024)S(1)}, u32[]{:S(2)}) copy-start(f32[1152]{0:T(1024)S(1)} %get-tuple-element.42) | copy-start | bytes 13828
  160.7 376.7 %copy-start.87 = (f32[1152]{0:T(1024)}, f32[1152]{0:T(1024)S(1)}, u32[]{:S(2)}) copy-start(f32[1152]{0:T(1024)S(1)} %get-tuple-element.40) | copy-start | bytes 13828
  160.7 554.9 %copy-start.50 = (f32[1152]{0:T(1024)}, f32[1152]{0:T(1024)S(1)}, u32[]{:S(2)}) copy-start(f32[1152]{0:T(1024)S(1)} %get-tuple-element.41) | copy-start | bytes 13828
  232.3 81.8 %all-gather.27.cloned.1.call-start = ((), (), s32[]{:S(2)}) async-start(), calls=%async_computation.20 | async-start | bytes 3538944 | tf_op jit(solution)/shard_map/all_gather | solution.py:116
  233.0 291.9 %copy-start.89 = (f32[1152]{0:T(1024)}, f32[1152]{0:T(1024)S(1)}, u32[]{:S(2)}) copy-start(f32[1152]{0:T(1024)S(1)} %get-tuple-element.34) | copy-start | bytes 13828
  233.0 481.9 %copy-start.53 = (f32[1152]{0:T(1024)}, f32[1152]{0:T(1024)S(1)}, u32[]{:S(2)}) copy-start(f32[1152]{0:T(1024)S(1)} %get-tuple-element.35) | copy-start | bytes 13828
  245.3 106.3 %all-gather.17.cloned.1.call-start = ((), (), s32[]{:S(2)}) async-start(), calls=%async_computation.15 | async-start | bytes 3538944 | tf_op jit(solution)/shard_map/all_gather | solution.py:116
  245.9 143.2 %all-gather.19.cloned.1.call-start = ((), (), s32[]{:S(2)}) async-start(), calls=%async_computation.16 | async-start | bytes 3538944 | tf_op jit(solution)/shard_map/all_gather | solution.py:115
  248.9 27.0 %copy-start.30 = (bf16[288,576]{1,0:T(8,128)(2,1)S(1)}, bf16[288,576]{1,0:T(8,128)(2,1)}, u32[]{:S(2)}) copy-start(bf16[288,576]{1,0:T(8,128)(2,1)} %param.30) | copy-start | bytes 995332
  248.9 186.3 %all-gather.21.cloned.1.call-start = ((), (), s32[]{:S(2)}) async-start(), calls=%async_computation.17 | async-start | bytes 2820096 | tf_op jit(solution)/shard_map/all_gather | solution.py:81
  258.0 266.8 %all-gather.23.cloned.1.call-start = ((), (), s32[]{:S(2)}) async-start(), calls=%async_computation.18 | async-start | bytes 11280384 | tf_op jit(solution)/shard_map/all_gather | solution.py:82
  275.9 338.8 %all-gather.25.cloned.1.call-start = ((), (), s32[]{:S(2)}) async-start(), calls=%async_computation.19 | async-start | bytes 11280384 | tf_op jit(solution)/shard_map/all_gather | solution.py:83
  288.0 707.9 %reduce-scatter.50.cloned.1.call-start = ((), (), s32[]{:S(2)}) async-start(), calls=%async_computation.35 | async-start | bytes 2820096
  481.6 234.0 %copy-start.65 = (f32[512]{0:T(512)}, f32[512]{0:T(512)S(1)}, u32[]{:S(2)}) copy-start(f32[512]{0:T(512)S(1)} %broadcast_multiply_fusion) | copy-start | bytes 6148
  482.0 232.9 %copy-start.67 = (f32[512]{0:T(512)}, f32[512]{0:T(512)S(1)}, u32[]{:S(2)}) copy-start(f32[512]{0:T(512)S(1)} %broadcast_multiply_fusion.2) | copy-start | bytes 6148
  483.9 231.8 %copy-start.77 = (f32[512]{0:T(512)}, f32[512]{0:T(512)S(1)}, u32[]{:S(2)}) copy-start(f32[512]{0:T(512)S(1)} %fusion.155) | copy-start | bytes 6148
  483.9 231.0 %copy-start.79 = (f32[512]{0:T(512)}, f32[512]{0:T(512)S(1)}, u32[]{:S(2)}) copy-start(f32[512]{0:T(512)S(1)} %fusion.153) | copy-start | bytes 6148
  537.4 77.2 %copy-start.100 = (f32[4608]{0:T(1024)S(1)}, f32[4608]{0:T(1024)}, u32[]{:S(2)}) copy-start(f32[4608]{0:T(1024)} %param.29) | copy-start | bytes 55300
  537.4 77.2 %copy-start.102 = (f32[1152]{0:T(1024)S(1)}, f32[1152]{0:T(1024)}, u32[]{:S(2)}) copy-start(f32[1152]{0:T(1024)} %param.31) | copy-start | bytes 13828
  546.5 82.0 %copy-start.91 = (f32[1152]{0:T(1024)S(1)}, f32[1152]{0:T(1024)}, u32[]{:S(2)}) copy-start(f32[1152]{0:T(1024)} %get-tuple-element.39) | copy-start | bytes 13828
  546.5 82.0 %copy-start.92 = (f32[1152]{0:T(1024)S(1)}, f32[1152]{0:T(1024)}, u32[]{:S(2)}) copy-start(f32[1152]{0:T(1024)} %get-tuple-element.33) | copy-start | bytes 13828
  744.3 253.7 %reduce-scatter.28.cloned.1.call-start = ((), (), s32[]{:S(2)}) async-start(), calls=%async_computation.23 | async-start | bytes 3538944 | tf_op jit(solution)/shard_map/reduce_scatter | solution.py:190
  787.9 210.1 %reduce-scatter.26.cloned.1.call-start = ((), (), s32[]{:S(2)}) async-start(), calls=%async_computation.22 | async-start | bytes 3538944 | tf_op jit(solution)/shard_map/reduce_scatter | solution.py:187
  788.0 28.3 %copy-start.18 = (bf16[1,512,1152]{1,2,0:T(8,128)(2,1)S(1)}, bf16[1,512,1152]{1,2,0:T(8,128)(2,1)}, u32[]{:S(2)}) copy-start(bf16[1,512,1152]{1,2,0:T(8,128)(2,1)} %copy.59) | copy-start | bytes 3538948
  826.6 183.9 %reduce-scatter.32.cloned.1.call-start = ((), (), s32[]{:S(2)}) async-start(), calls=%async_computation.25 | async-start | bytes 3538944 | tf_op jit(solution)/shard_map/reduce_scatter | solution.py:190
  864.9 145.7 %reduce-scatter.30.cloned.1.call-start = ((), (), s32[]{:S(2)}) async-start(), calls=%async_computation.24 | async-start | bytes 3538944 | tf_op jit(solution)/shard_map/reduce_scatter | solution.py:187
  864.9 28.7 %copy-start.17 = (bf16[1,512,1152]{1,2,0:T(8,128)(2,1)S(1)}, bf16[1,512,1152]{1,2,0:T(8,128)(2,1)}, u32[]{:S(2)}) copy-start(bf16[1,512,1152]{1,2,0:T(8,128)(2,1)} %copy.64) | copy-start | bytes 3538948
  904.0 174.5 %reduce-scatter.38.cloned.1.call-start = ((), (), s32[]{:S(2)}) async-start(), calls=%async_computation.29 | async-start | bytes 11280384 | tf_op jit(solution)/shard_map/reduce_scatter | solution.py:232
  937.1 265.9 %reduce-scatter.34.cloned.1.call-start = ((), (), s32[]{:S(2)}) async-start(), calls=%async_computation.27 | async-start | bytes 11280384 | tf_op jit(solution)/shard_map/reduce_scatter | solution.py:229
  967.0 250.6 %reduce-scatter.42.cloned.1.call-start = ((), (), s32[]{:S(2)}) async-start(), calls=%async_computation.31 | async-start | bytes 442368
  997.7 325.2 %reduce-scatter.48.cloned.1.call-start = ((), (), s32[]{:S(2)}) async-start(), calls=%async_computation.34 | async-start | bytes 8460288
  1025.4 402.7 %reduce-scatter.46.cloned.1.call-start = ((), (), s32[]{:S(2)}) async-start(), calls=%async_computation.33 | async-start | bytes 8460288
  1073.7 130.9 %copy-start.83 = (f32[1152]{0:T(1024)S(1)}, f32[1152]{0:T(1024)}, u32[]{:S(2)}) copy-start(f32[1152]{0:T(1024)} %get-tuple-element.61) | copy-start | bytes 13828
  1073.7 130.9 %copy-start.84 = (f32[1152]{0:T(1024)S(1)}, f32[1152]{0:T(1024)}, u32[]{:S(2)}) copy-start(f32[1152]{0:T(1024)} %get-tuple-element.87) | copy-start | bytes 13828
  1073.7 375.0 %reduce-scatter.44.cloned.1.call-start = ((), (), s32[]{:S(2)}) async-start(), calls=%async_computation.32 | async-start | bytes 1327104
  1080.9 386.2 %reduce-scatter.36.cloned.1.call-start = ((), (), s32[]{:S(2)}) async-start(), calls=%async_computation.28 | async-start | bytes 995328 | tf_op jit(solution)/shard_map/reduce_scatter | solution.py:243
  1203.0 284.9 %reduce-scatter.40.cloned.1.call-start = ((), (), s32[]{:S(2)}) async-start(), calls=%async_computation.30 | async-start | bytes 1327104
  1325.2 289.4 %all-reduce.7.cloned.1.call-start = ((), (), s32[]{:S(2)}) async-start(), calls=%async_computation.26 | async-start | bytes 221184 | tf_op jit(solution)/shard_map/psum | solution.py:250
  1428.1 188.1 %copy-start.1 = (f32[24,1152]{1,0:T(8,128)S(1)}, f32[24,1152]{1,0:T(8,128)}, u32[]{:S(2)}) copy-start(f32[24,1152]{1,0:T(8,128)} %param.17) | copy-start | bytes 331780
  (85 other events, 714.0 us)
Sparse Core Ops, SparseCore 0:
  25.5 121.8 all-gather.12
  150.1 70.3 all-gather.14
  232.4 43.4 all-gather.28
  277.9 36.1 all-gather.26
  315.5 36.0 all-gather.16
  353.0 36.0 all-gather.18
  391.8 43.3 all-gather.20
  437.5 87.3 all-gather.22
  527.7 86.8 all-gather.24
  744.4 62.0 reduce-scatter.49
  808.8 33.6 reduce-scatter.27
  844.6 34.7 reduce-scatter.25
  881.7 34.7 reduce-scatter.31
  919.1 34.6 reduce-scatter.29
  958.3 120.2 reduce-scatter.37
  1083.0 119.9 reduce-scatter.33
  1205.7 11.7 reduce-scatter.41
  1222.0 100.8 reduce-scatter.47
  1327.0 101.0 reduce-scatter.45
  1430.3 18.2 reduce-scatter.43
  1451.0 16.0 reduce-scatter.35
  1469.4 18.5 reduce-scatter.39
  1494.1 120.5 all-reduce.6
where the time goes:
time: 1630 us; the launch traced here: 1620 us
  waiting for transfers between devices  814 us (50%)
  matrix products  486 us (30%)
  blocking collectives  123 us (8%)
  other arithmetic  113 us (7%)
  local copies, waits for them, and re-layouts  66.5 us (4%)
  between operations  19.3 us (1%)
    unnamed x29, waiting for transfers between devices  182 us
    psum x1, waiting for transfers between devices, local(): lax.psum((loss_sum, bias_ada, bias_qv, bias_proj, bias_fc1, bias_fc2, gra...  125 us
    reduce_scatter x1, waiting for transfers between devices, local(): lax.psum_scatter(grad_fc1.astype(jnp.bfloat16), 'dp', scatter_dimension=0...  122 us
    all_gather x1, waiting for transfers between devices, local(): ada_full = lax.all_gather(ada_cols, 'dp', axis=0, tiled=True)  105 us
    all_gather x1, waiting for transfers between devices, local(): fc2_full = lax.all_gather(fc2_cols, 'dp', axis=0, tiled=True)  68.1 us
    all_gather x1, waiting for transfers between devices, local(): qkv_full = lax.all_gather(qkv_cols, 'dp', axis=0, tiled=True)  59.7 us
    convert_element_type x2, other arithmetic, local(): d_scores = (probs * (d_probs - row_inner)).astype(bf16)  56.9 us
    all_gather x2, waiting for transfers between devices, local(): lax.all_gather(values_local, 'seq', axis=1, tiled=True)  48.2 us
  transfers between devices with their start and end apart: 23, of which 17 were waited for; matrix products, arithmetic and copies ran while one was open for 31% of the time, Pallas kernels for 0%

commit v1 on v0

v1 whole, which is shorter than its diff:
```python
import functools

import jax
import jax.numpy as jnp
from jax import lax
from jax.experimental import pallas as pl
from jax.experimental.pallas import tpu as pltpu
from jax.sharding import PartitionSpec as P

HEADS = 16
HIGH = lax.Precision.HIGHEST
LOG2E = 1.4426950408889634
F32 = jnp.float32
BF16 = jnp.bfloat16
NT = (((1,), (1,)), ((), ()))
NN = (((1,), (0,)), ((), ()))
TN = (((0,), (0,)), ((), ()))


def dot(a, b, dims=NN):
    return lax.dot_general(a, b, dims, preferred_element_type=F32)


def params(**kw):
    return pltpu.CompilerParams(vmem_limit_bytes=56 * 2**20, **kw)


def attn_fwd_kernel(heads, hs, coef, q_ref, kv_ref, o_ref, lse_ref, qs, ks, vt, os):
    width = heads * hs
    for h in range(heads):
        cols = slice(h * hs, (h + 1) * hs)
        qs[h] = q_ref[0, :, cols]
        ks[h] = kv_ref[0, :, cols]
        vt[h] = kv_ref[0, :, width + h * hs : width + (h + 1) * hs].T

    def head(h, carry):
        scores = dot(ks[h], qs[h], NT)
        top = jnp.max(scores, axis=0, keepdims=True)
        probs = jnp.exp2((scores - top) * coef)
        total = jnp.sum(probs, axis=0, keepdims=True)
        out = dot(vt[h], probs.astype(BF16)) / total
        os[h] = out.T.astype(BF16)
        lse_ref[0, h] = top * coef + jnp.log2(total)
        return carry

    lax.fori_loop(0, heads, head, 0)
    for h in range(heads):
        o_ref[0, :, h * hs : (h + 1) * hs] = os[h]


def attn_fwd(q, kv, heads):
    batch, lq, width = q.shape
    lk = kv.shape[1]
    hs = width // heads
    return pl.pallas_call(
        functools.partial(attn_fwd_kernel, heads, hs, hs**-0.5 * LOG2E),
        grid=(batch,),
        in_specs=[
            pl.BlockSpec((1, lq, width), lambda b: (b, 0, 0)),
            pl.BlockSpec((1, lk, 2 * width), lambda b: (b, 0, 0)),
        ],
        out_specs=[
            pl.BlockSpec((1, lq, width), lambda b: (b, 0, 0)),
            pl.BlockSpec((1, heads, 1, lq), lambda b: (b, 0, 0, 0)),
        ],
        out_shape=[
            jax.ShapeDtypeStruct((batch, lq, width), BF16),
            jax.ShapeDtypeStruct((batch, heads, 1, lq), F32),
        ],
        scratch_shapes=[
            pltpu.VMEM((heads, lq, hs), BF16),
            pltpu.VMEM((heads, lk, hs), BF16),
            pltpu.VMEM((heads, hs, lk), BF16),
            pltpu.VMEM((heads, lq, hs), BF16),
        ],
        compiler_params=params(),
        cost_estimate=pl.CostEstimate(
            flops=4 * batch * lq * lk * width,
            transcendentals=batch * heads * lq * lk,
            bytes_accessed=batch * width * (4 * lq + 4 * lk),
        ),
        name="attn_fwd",
    )(q, kv)


def attn_bwd_kernel(
    heads, hs, coef, scale, q_ref, kv_ref, do_ref, lse_ref, dq_ref, dkv_ref, qs, ks, kt, vs, ds, dks, dvs
):
    width = heads * hs
    for h in range(heads):
        cols = slice(h * hs, (h + 1) * hs)
        qs[h] = q_ref[0, :, cols]
        ds[h] = do_ref[0, :, cols]
        key = kv_ref[0, :, cols]
        ks[h] = key
        kt[h] = key.T
        vs[h] = kv_ref[0, :, width + h * hs : width + (h + 1) * hs]

    def head(h, carry):
        query, grad = qs[h], ds[h]
        probs = jnp.exp2(dot(ks[h], query, NT) * coef - lse_ref[0, h])
        dvs[h] = dot(probs.astype(BF16), grad).astype(BF16)
        weighted = probs * dot(vs[h], grad, NT)
        inner = jnp.sum(weighted, axis=0, keepdims=True)
        dscore = (weighted - probs * inner).astype(BF16)
        dks[h] = (dot(dscore, query) * scale).astype(BF16)
        qs[h] = (dot(kt[h], dscore) * scale).T.astype(BF16)
        return carry

    lax.fori_loop(0, heads, head, 0)
    for h in range(heads):
        cols = slice(h * hs, (h + 1) * hs)
        dq_ref[0, :, cols] = qs[h]
        dkv_ref[0, :, cols] = dks[h]
        dkv_ref[0, :, width + h * hs : width + (h + 1) * hs] = dvs[h]


def attn_bwd(q, kv, grad, lse, heads):
    batch, lq, width = q.shape
    lk = kv.shape[1]
    hs = width // heads
    row = pl.BlockSpec((1, lq, width), lambda b: (b, 0, 0))
    wide = pl.BlockSpec((1, lk, 2 * width), lambda b: (b, 0, 0))
    return pl.pallas_call(
        functools.partial(attn_bwd_kernel, heads, hs, hs**-0.5 * LOG2E, hs**-0.5),
        grid=(batch,),
        in_specs=[row, wide, row, pl.BlockSpec((1, heads, 1, lq), lambda b: (b, 0, 0, 0))],
        out_specs=[row, wide],
        out_shape=[
            jax.ShapeDtypeStruct((batch, lq, width), BF16),
            jax.ShapeDtypeStruct((batch, lk, 2 * width), BF16),
        ],
        scratch_shapes=[
            pltpu.VMEM((heads, lq, hs), BF16),
            pltpu.VMEM((heads, lk, hs), BF16),
            pltpu.VMEM((heads, hs, lk), BF16),
            pltpu.VMEM((heads, lk, hs), BF16),
            pltpu.VMEM((heads, lq, hs), BF16),
            pltpu.VMEM((heads, lk, hs), BF16),
            pltpu.VMEM((heads, lk, hs), BF16),
        ],
        compiler_params=params(),
        cost_estimate=pl.CostEstimate(
            flops=10 * batch * lq * lk * width,
            transcendentals=batch * heads * lq * lk,
            bytes_accessed=batch * width * (8 * lq + 8 * lk),
        ),
        name="attn_bwd",
    )(q, kv, grad, lse)


def norm_parts(value):
    center = value - jnp.mean(value, axis=-1, keepdims=True)
    spread = jnp.mean(center * center, axis=-1, keepdims=True)
    inv = lax.rsqrt(spread + 1e-06)
    return center * inv, inv


def norm_grad(normed, inv, grad):
    first = jnp.mean(grad, axis=-1, keepdims=True)
    second = jnp.mean(grad * normed, axis=-1, keepdims=True)
    return inv * (grad - first - normed * second)


def gelu_tanh(value):
    return jax.nn.gelu(value, approximate=True)


def scatter(grad):
    rows = lax.psum_scatter(grad.astype(BF16), "dp", scatter_dimension=0, tiled=True)
    return lax.psum_scatter(rows, "seq", scatter_dimension=1, tiled=True).astype(F32)


def gather(weight):
    return lax.all_gather(
        lax.all_gather(weight, "seq", axis=1, tiled=True), "dp", axis=0, tiled=True
    )


def local(
    latents,
    cond,
    slot_mask,
    slot_image,
    teacher,
    cotangent,
    ada_w,
    ada_b,
    qkv_w,
    qv_b,
    proj_w,
    proj_b,
    fc1_w,
    fc1_b,
    fc2_w,
    fc2_b,
):
    micro, slots_dev, length, width = latents.shape
    images = cond.shape[0]
    nd, ns = lax.axis_size("dp"), lax.axis_size("seq")
    dp_index, seq_index = lax.axis_index("dp"), lax.axis_index("seq")
    batch = micro * slots_dev
    tokens = batch * length
    full = length * ns
    rows_dev, mod_cols = ada_w.shape
    count = jnp.sum(slot_mask).astype(F32) * full
    divisor = count * width

    lat = latents.reshape(batch, length, width)
    lat_all = lax.all_gather(lat, "seq", axis=1, tiled=True)
    qkv = gather(qkv_w)
    proj = gather(proj_w)
    fc1 = gather(fc1_w)
    fc2 = gather(fc2_w)

    image_table = jnp.arange(images, dtype=jnp.int32)
    by_dev = slot_image.reshape(micro, nd, slots_dev).transpose(1, 0, 2).reshape(nd * batch)
    pick = (by_dev[:, None] == image_table[None, :]).astype(F32)
    cond_all = jnp.dot(pick, cond, precision=HIGH)
    cond_own = lax.dynamic_slice_in_dim(cond_all, dp_index * rows_dev, rows_dev, 1)
    silu_own = jax.nn.silu(cond_own).astype(BF16)
    mod_part = lax.psum_scatter(dot(silu_own, ada_w), "dp", scatter_dimension=0, tiled=True)
    modulation = lax.all_gather(mod_part, "seq", axis=1, tiled=True) + ada_b
    pieces = [modulation[:, i * width : (i + 1) * width][:, None, :] for i in range(6)]
    shift1, scale1, gate1, shift2, scale2, gate2 = pieces

    normed_all, inv_all = norm_parts(lat_all.astype(F32))
    hidden_all = (normed_all * (1.0 + scale1) + shift1).astype(BF16)
    own = lambda value: lax.dynamic_slice_in_dim(value, seq_index * length, length, 1)
    hidden = own(hidden_all)
    inputs = lat.astype(F32)
    flat = lambda value: value.reshape(-1, value.shape[-1])
    wide = lambda value: value.reshape(batch, -1, value.shape[-1])

    query = (dot(flat(hidden), qkv[:, :width]) + qv_b[:width]).astype(BF16)
    kv_bias = jnp.concatenate([jnp.zeros((width,), F32), qv_b[width:]])
    kv = (dot(flat(hidden_all), qkv[:, width:]) + kv_bias).astype(BF16)
    query, kv = wide(query), wide(kv)
    attended, lse = attn_fwd(query, kv, HEADS)

    branch = wide(dot(flat(attended), proj) + proj_b)
    middle = inputs + gate1 * branch
    normed2, inv2 = norm_parts(middle)
    hidden2 = flat((normed2 * (1.0 + scale2) + shift2).astype(BF16))
    before = dot(hidden2, fc1) + fc1_b
    active = gelu_tanh(before).astype(BF16)
    mlp_out = wide(dot(active, fc2) + fc2_b)
    result = middle + gate2 * mlp_out
    block_out = result.astype(BF16).reshape(latents.shape)

    mask_mine = lax.dynamic_slice_in_dim(slot_mask, dp_index * slots_dev, slots_dev, 1)
    valid = mask_mine.reshape(batch, 1, 1).astype(F32)
    diff = result - teacher.reshape(lat.shape).astype(F32)
    loss_sum = jnp.sum(valid * diff * diff)
    grad_out = valid * (2.0 * diff / divisor + cotangent.reshape(lat.shape).astype(F32))
    d_gate2 = jnp.sum(grad_out * mlp_out, axis=1)
    d_mlp = flat((grad_out * gate2).astype(BF16))
    grad_fc2 = dot(active, d_mlp, TN)
    fc2_w_grad = scatter(grad_fc2)
    bias_fc2 = jnp.sum(d_mlp.astype(F32), axis=0)
    d_active = dot(d_mlp, fc2, NT)
    d_before = jax.vjp(gelu_tanh, before)[1](d_active)[0].astype(BF16)
    grad_fc1 = dot(hidden2, d_before, TN)
    fc1_w_grad = scatter(grad_fc1)
    bias_fc1 = jnp.sum(d_before.astype(F32), axis=0)
    d_hidden2 = wide(dot(d_before, fc1, NT))
    d_scale2 = jnp.sum(d_hidden2 * normed2, axis=1)
    d_shift2 = jnp.sum(d_hidden2, axis=1)
    d_middle = grad_out + norm_grad(normed2, inv2, d_hidden2 * (1.0 + scale2))
    d_gate1 = jnp.sum(d_middle * branch, axis=1)
    d_branch = flat((d_middle * gate1).astype(BF16))
    grad_proj = dot(flat(attended), d_branch, TN)
    proj_w_grad = scatter(grad_proj)
    bias_proj = jnp.sum(d_branch.astype(F32), axis=0)
    d_attended = wide(dot(d_branch, proj, NT).astype(BF16))

    d_query, d_kv = attn_bwd(query, kv, d_attended, lse, HEADS)
    d_query, d_kv = flat(d_query), flat(d_kv)
    grad_q = dot(flat(hidden), d_query, TN)
    grad_kv = dot(flat(hidden_all), d_kv, TN)
    qkv_w_grad = scatter(jnp.concatenate([grad_q, grad_kv], axis=1))
    bias_qv = jnp.concatenate(
        [jnp.sum(d_query.astype(F32), axis=0), jnp.sum(d_kv[:, width:].astype(F32), axis=0)]
    )
    dh_q = wide(dot(d_query, qkv[:, :width], NT))
    dh_kv = wide(dot(d_kv, qkv[:, width:], NT))
    others = lax.psum_scatter(dh_kv.astype(BF16), "seq", scatter_dimension=1, tiled=True)
    d_hidden = dh_q + others.astype(F32)
    normed1, inv1 = own(normed_all), own(inv_all)
    d_scale1 = jnp.sum(dh_kv * normed_all, axis=1) + jnp.sum(dh_q * normed1, axis=1)
    d_shift1 = jnp.sum(dh_kv, axis=1) + jnp.sum(dh_q, axis=1)
    d_inputs = d_middle + norm_grad(normed1, inv1, d_hidden * (1.0 + scale1))
    latents_grad = d_inputs.reshape(latents.shape)

    mod_partial = jnp.concatenate([d_shift1, d_scale1, d_gate1, d_shift2, d_scale2, d_gate2], axis=-1)
    d_mod = lax.psum(mod_partial, "seq").astype(BF16)
    col_start = seq_index * mod_cols
    own_cols = lax.dynamic_slice_in_dim(d_mod, col_start, mod_cols, 1)
    d_mod_all = lax.all_gather(own_cols, "dp", axis=0, tiled=True)
    ada_w_grad = dot(silu_own, d_mod_all, TN)
    bias_ada = lax.dynamic_update_slice(
        jnp.zeros((6 * width,), F32), jnp.sum(own_cols.astype(F32), axis=0), (col_start,)
    )
    d_cond = dot(d_mod_all, ada_w, NT)
    d_cond = jax.vjp(jax.nn.silu, cond_own)[1](d_cond)[0]
    grad_cond = lax.dynamic_update_slice(
        jnp.zeros((images, width), F32),
        lax.dot_general(pick, d_cond, TN, precision=HIGH),
        (0, dp_index * rows_dev),
    )
    summed = lax.psum(
        (loss_sum, bias_ada, bias_qv, bias_proj, bias_fc1, bias_fc2, grad_cond), ("dp", "seq")
    )
    return (
        block_out,
        latents_grad,
        summed[0] / divisor,
        summed[6],
        ada_w_grad,
        summed[1],
        qkv_w_grad,
        summed[2],
        proj_w_grad,
        summed[3],
        fc1_w_grad,
        summed[4],
        fc2_w_grad,
        summed[5],
    )


def solution(mesh):
    tokens = P(None, "dp", "seq", None)
    both = P("dp", "seq")
    return jax.shard_map(
        local,
        mesh=mesh,
        in_specs=(tokens, P(), P(), P(), tokens, tokens, both, P(), both, P(), both, P(), both, P(), both, P()),
        out_specs=(tokens, tokens, P(), P(), both, P(), both, P(), both, P(), both, P(), both, P()),
        check_vma=False,
    )
```

time: 1630 us -> 1210 us (0.74)
  matrix products: 486 us -> 236 us
  waiting for transfers between devices: 814 us -> 568 us
  Pallas kernels: 0 us -> 146 us
  other arithmetic: 113 us -> 65.6 us
  local copies, waits for them, and re-layouts: 66.5 us -> 40.8 us
    dot_general x40 -> x20, matrix products: 451 us -> 236 us  [the longest x18 234 us: dot(): return lax.dot_general(a, b, dims, preferred_element_type=F32)]
    all_gather x9 -> x5, waiting for transfers between devices: 365 us -> 162 us  [the longest x4 162 us: gather(): lax.all_gather(lax.all_gather(weight, 'seq', axis=1, tiled=True), 'dp', a...]
    pallas_call x0 -> x2, Pallas kernels: none -> 146 us  [the longest x1 87.8 us: attn_bwd(): pl.pallas_call(functools.partial(attn_bwd_kernel, heads, hs, hs ** (-0.5)...]
    reduce_scatter x7 -> x4, waiting for transfers between devices: 143 us -> 287 us  [the longest x2 227 us: scatter(): lax.psum_scatter(grad.astype(BF16), 'dp', scatter_dimension=0, tiled=True)]
    unnamed x29 -> x22, waiting for transfers between devices: 182 us -> 51 us
    convert_element_type x10 -> x8, other arithmetic: 73.1 us -> 15.4 us  [the longest x1 6.14 us: local(): cotangent.reshape(lat.shape).astype(F32)]
    psum x1, waiting for transfers between devices: 125 us -> 68.1 us  [local(): lax.psum((loss_sum, bias_ada, bias_qv, bias_proj, bias_fc1, bias_fc2, gra...]
    sub x2 -> x0, matrix products: 35.3 us -> none  [local(): probs_low = (jnp.exp(scores - row_top) / row_total).astype(bf16)]
  transfers between devices with their start and end apart: 23 -> 16, of which waited for: 17 -> 9; matrix products, arithmetic and copies ran while one was open for 31% -> 18% of each run, Pallas kernels for 0% -> 12%
where the time goes in v1:
time: 1210 us
  waiting for transfers between devices  568 us (47%)
  matrix products  236 us (20%)
  Pallas kernels  146 us (12%)
  blocking collectives  129 us (11%)
  other arithmetic  65.6 us (5%)
  local copies, waits for them, and re-layouts  40.8 us (3%)
  between operations  20 us (2%)
    dot_general x18, matrix products, dot(): return lax.dot_general(a, b, dims, preferred_element_type=F32)  234 us
    reduce_scatter x2, waiting for transfers between devices, scatter(): lax.psum_scatter(grad.astype(BF16), 'dp', scatter_dimension=0, tiled=True)  227 us
    all_gather x4, waiting for transfers between devices, gather(): lax.all_gather(lax.all_gather(weight, 'seq', axis=1, tiled=True), 'dp', a...  162 us
    pallas_call x1, Pallas kernels, attn_bwd(): pl.pallas_call(functools.partial(attn_bwd_kernel, heads, hs, hs ** (-0.5)...  87.8 us
    psum x1, waiting for transfers between devices, local(): lax.psum((loss_sum, bias_ada, bias_qv, bias_proj, bias_fc1, bias_fc2, gra...  68.1 us
    reduce_scatter x1, waiting for transfers between devices, local(): lax.psum_scatter(dh_kv.astype(BF16), 'seq', scatter_dimension=1, tiled=True)  59.5 us
    pallas_call x1, Pallas kernels, attn_fwd(): pl.pallas_call(functools.partial(attn_fwd_kernel, heads, hs, hs ** (-0.5)...  57.9 us
    all_gather x4, blocking collectives, gather(): lax.all_gather(weight, 'seq', axis=1, tiled=True)  56.1 us
  transfers between devices with their start and end apart: 16, of which 9 were waited for; matrix products, arithmetic and copies ran while one was open for 18% of the time, Pallas kernels for 12%

profile of v1, /device:TPU:0, one launch (start us, length us, event | category | flops | bytes accessed | tf_op | source)
XLA Modules:
  0.0 1206.5 jit_solution(9884919845028452895)
XLA Ops:
  12.5 10.1 all-gather.1
  24.3 7.1 all-gather.2
  32.5 20.0 %all_gather.39 = bf16[72,4608]{1,0:T(8,128)(2,1)} all-gather(bf16[72,2304]{1,0:T(8,128)(2,1)} %param.28), channel_id=1, replica_groups=mesh['dp'=16,'seq'=2] {'seq'}, dimensions={1}, use_global_device_ids=true | all-gather | bytes 995328 | tf_op jit(solution)/shard_map/all_gather | solution.py:176
  52.6 18.9 %all-gather.3 = bf16[2,576,288]{1,2,0:T(8,128)(2,1)S(1)} all-gather(bf16[1,576,288]{1,2,0:T(8,128)(2,1)} %bitcast.273), channel_id=1, replica_groups=mesh['dp'=16,'seq'=2] {'seq'}, dimensions={0}, use_global_device_ids=true | all-gather | bytes 995328 | tf_op jit(solution)/shard_map/all_gather | solution.py:176
  72.9 2.8 reshape.286
  78.6 6.1 bitcast_convert_fusion
  84.8 20.5 %all-reduce.10.cloned.1.call-done = f32[32,3456]{1,0:T(8,128)} async-done(((f32[32,3456]{1,0:T(8,128)}), f32[32,3456]{1,0:T(8,128)}) %all-reduce.10.cloned.1.call-update) | async-done | bytes 442384
  106.2 4.5 all_gather.33
  110.9 3.2 convert_reduce_fusion.1
  120.6 49.6 %all-gather.11.cloned.1.call-done = bf16[1152,3456]{1,0:T(8,128)(2,1)} async-done(((bf16[72,3456]{1,0:T(8,128)(2,1)}), bf16[1152,3456]{1,0:T(8,128)(2,1)}) %all-gather.11.cloned.1.call-update) | async-done | bytes 7962640 | tf_op jit(solution)/shard_map/all_gather | solution.py:175
  170.2 6.6 add_convert_fusion.3
  176.8 14.3 %add_convert_fusion = bf16[2048,2304]{1,0:T(8,128)(2,1)} fusion(bf16[2048,1152]{1,0:T(8,128)(2,1)S(1)} %bitcast.262, f32[2304]{0:T(1024)S(1)} %concatenate.13, bf16[1152,3456]{1,0:T(8,128)(2,1)S(1)} %copy-done.46), kind=kOutput, calls=%fused_computation.13 | convolution fusion | flops 10881073152 | bytes 19476480 | tf_op jit(solution)/shard_map/dot_general | solution.py:21
  191.2 57.9 %attn_fwd.1 = (bf16[2,512,1152]{2,1,0:T(8,128)(2,1)}, f32[2,16,1,512]{3,2,1,0:T(1,128)}) custom-call(bf16[2,512,1152]{2,1,0:T(8,128)(2,1)} %bitcast.287, bf16[2,1024,2304]{2,1,0:T(8,128)(2,1)} %bitcast.285), custom_call_target="tpu_custom_call" | custom-call | flops 4831838208 | bytes 14155776 | tf_op jit(solution)/shard_map/attn_fwd/pallas_call | solution.py:55
  249.1 6.1 convolution_add_fusion.1
  256.1 2.6 copy-done.5
  259.3 2.6 fusion.20
  261.9 42.4 %all-gather.15.cloned.1.call-done = bf16[1152,4608]{1,0:T(8,128)(2,1)} async-done(((bf16[72,4608]{1,0:T(8,128)(2,1)}), bf16[1152,4608]{1,0:T(8,128)(2,1)}) %all-gather.15.cloned.1.call-update) | async-done | bytes 10616848 | tf_op jit(solution)/shard_map/all_gather | solution.py:175
  304.3 19.4 %fusion.67 = f32[1024,4608]{1,0:T(8,128)} fusion(bf16[1024,1152]{1,0:T(8,128)(2,1)} %fusion.20, bf16[1152,4608]{1,0:T(8,128)(2,1)} %all-gather.15.cloned.1.call-done), kind=kOutput, calls=%fused_computation.140 | convolution fusion | flops 10871635968 | bytes 31850496 | tf_op jit(solution)/shard_map/dot_general | solution.py:21
  323.7 70.1 %all-gather.17.cloned.1.call-done = bf16[4608,1152]{1,0:T(8,128)(2,1)} async-done(((bf16[288,1152]{1,0:T(8,128)(2,1)}), bf16[4608,1152]{1,0:T(8,128)(2,1)}) %all-gather.17.cloned.1.call-update) | async-done | bytes 10616848 | tf_op jit(solution)/shard_map/all_gather | solution.py:175
  393.8 27.4 %convert_reduce_fusion.3 = (f32[1152]{0:T(1024)}, bf16[1024,1152]{1,0:T(8,128)(2,1)}, f32[1024,1152]{1,0:T(8,128)}, f32[1024,1152]{1,0:T(8,128)}) fusion(f32[2,1152]{1,0:T(2,128)S(1)} %get-tuple-element.97, f32[2,1,512,1152]{3,2,0,1:T(8,128)} %get-tuple-element.113, f32[]{:T(128)S(6)} %mul.348, f32[2,1,512,1152]{3,2,0,1:T(8,128)} %get-tuple-element.114, ...), kind=kOutput, calls=%fused_computation.59 | convolution fusion | flops 10936515584 | bytes 57852932 | tf_op jit(solution)/shard_map/dot_general | solution.py:21
  421.2 27.2 %convert_reduce_fusion = (f32[4608]{0:T(1024)}, bf16[1024,4608]{1,0:T(8,128)(2,1)}) fusion(f32[1024,4608]{1,0:T(8,128)} %fusion.67, f32[4608]{0:T(1024)S(1)} %copy-done.39, bf16[1024,1152]{1,0:T(8,128)(2,1)} %get-tuple-element.83, bf16[4608,1152]{1,0:T(8,128)(2,1)S(1)} %copy-done.11), kind=kOutput, calls=%fused_computation.11 | convolution fusion | flops 10980159488 | bytes 41324544 | tf_op jit(solution)/shard_map/dot_general | solution.py:21
  448.4 20.8 %fusion.32 = (f32[1024]{0:T(1024)S(1)}, f32[1024]{0:T(1024)S(1)}, f32[1024,1152]{1,0:T(8,128)}) fusion(f32[2,1152]{1,0:T(2,128)S(1)} %get-tuple-element.99, f32[1024]{0:T(1024)S(1)} %bitcast.278, f32[1024]{0:T(1024)S(1)} %bitcast.281, f32[1024,1152]{1,0:T(8,128)} %copy-done.1, f32[2,1152]{1,0:T(2,128)S(1)} %get-tuple-element.102, ...), kind=kOutput, calls=%fused_computation.78 | convolution fusion | flops 10882250752 | bytes 31885312 | tf_op jit(solution)/shard_map/dot_general | solution.py:21
  469.3 8.1 convert_reduce_fusion.4
  479.4 9.1 multiply_reduce_fusion.1
  490.7 6.7 fusion.13
  497.4 6.6 convolution_convert_fusion.2
  504.0 87.8 %attn_bwd.1 = (bf16[2,512,1152]{2,1,0:T(8,128)(2,1)}, bf16[2,1024,2304]{2,1,0:T(8,128)(2,1)}) custom-call(bf16[2,512,1152]{2,1,0:T(8,128)(2,1)} %bitcast.288, bf16[2,1024,2304]{2,1,0:T(8,128)(2,1)} %bitcast.286, bf16[2,512,1152]{2,1,0:T(8,128)(2,1)} %bitcast.290, f32[2,16,1,512]{3,2,1,0:T(1,128)} %get-tuple-element.19.lse_ref), custom_call_target="tpu_custom_call" | custom-call | flops 12079595520 | bytes 28311552 | tf_op jit(solution)/shard_map/attn_bwd/pallas_call | solution.py:124
  591.9 6.5 fusion.12
  598.3 4.1 copy.66
  602.5 17.1 %fusion.7 = bf16[1152,2304]{1,0:T(8,128)(2,1)} fusion(bf16[2,1024,1152]{2,1,0:T(8,128)(2,1)} %copy-done.9, bf16[2,1024,2304]{2,1,0:T(8,128)(2,1)} %get-tuple-element.21), kind=kOutput, calls=%fused_computation.17 | convolution fusion | flops 10874290176 | bytes 19464192 | tf_op jit(solution)/shard_map/dot_general | solution.py:21
  621.5 6.3 pad_maximum_fusion
  628.5 20.5 %multiply_reduce_fusion = (f32[2,1152]{1,0:T(2,128)S(1)}, f32[2,1152]{1,0:T(2,128)S(1)}, bf16[2,1024,1152]{2,1,0:T(8,128)(2,1)}, f32[2,1024,1152]{2,1,0:T(8,128)}) fusion(f32[2,1024]{1,0:T(2,128)S(1)} %copy-done.29, f32[2,1024]{1,0:T(2,128)S(1)} %copy-done.27, bf16[2,1,1024,1152]{3,2,0,1:T(8,128)(2,1)} %all-gather.19.cloned.1.call-done, ...), kind=kOutput, calls=%fused_computation.23 | convolution fusion | flops 10888146944 | bytes 33654784 | tf_op jit(solution)/shard_map/dot_general | solution.py:21
  651.0 23.5 %convolution_convert_fusion = bf16[4608,1152]{1,0:T(8,128)(2,1)} fusion(bf16[1024,1152]{1,0:T(8,128)(2,1)S(1)} %copy-done.16, f32[1024,4608]{1,0:T(8,128)} %fusion.67, f32[4608]{0:T(1024)S(1)} %copy-done.39), kind=kOutput, calls=%fused_computation.2 | convolution fusion | flops 10924130304 | bytes 31868928 | tf_op jit(solution)/shard_map/dot_general | solution.py:21
  676.2 17.2 %convolution_convert_fusion.1 = bf16[1152,4608]{1,0:T(8,128)(2,1)} fusion(bf16[1024,1152]{1,0:T(8,128)(2,1)S(1)} %copy-done.20, bf16[1024,4608]{1,0:T(8,128)(2,1)} %get-tuple-element.86), kind=kOutput, calls=%fused_computation.3 | convolution fusion | flops 10876944384 | bytes 22413312 | tf_op jit(solution)/shard_map/dot_general | solution.py:21
  696.0 3.2 convert_reduce_fusion.2
  699.2 6.4 fusion.35
  707.4 29.7 %reduce-scatter.34.cloned.1.call-done = bf16[72,3456]{1,0:T(8,128)(2,1)} async-done(((bf16[1152,3456]{1,0:T(8,128)(2,1)}), bf16[72,3456]{1,0:T(8,128)(2,1)}) %reduce-scatter.34.cloned.1.call-update) | async-done | bytes 497680
  737.0 2.3 copy.73
  739.4 59.5 %reduce-scatter.20.cloned.1.call-done = bf16[2,512,1152]{2,1,0:T(8,128)(2,1)} async-done(((bf16[2,1024,1152]{2,1,0:T(8,128)(2,1)}), bf16[2,512,1152]{2,1,0:T(8,128)(2,1)}) %reduce-scatter.20.cloned.1.call-update) | async-done | bytes 2359312 | tf_op jit(solution)/shard_map/reduce_scatter | solution.py:287
  798.9 10.6 multiply_reduce_fusion.3
  809.5 114.2 %reduce-scatter.26.cloned.1.call-done = bf16[288,1152]{1,0:T(8,128)(2,1)} async-done(((bf16[4608,1152]{1,0:T(8,128)(2,1)}), bf16[288,1152]{1,0:T(8,128)(2,1)}) %reduce-scatter.26.cloned.1.call-update) | async-done | bytes 663568 | tf_op jit(solution)/shard_map/reduce_scatter | solution.py:170
  923.7 2.3 copy.77
  926.2 9.0 psum.57
  935.1 113.2 %reduce-scatter.22.cloned.1.call-done = bf16[72,4608]{1,0:T(8,128)(2,1)} async-done(((bf16[1152,4608]{1,0:T(8,128)(2,1)}), bf16[72,4608]{1,0:T(8,128)(2,1)}) %reduce-scatter.22.cloned.1.call-update) | async-done | bytes 663568 | tf_op jit(solution)/shard_map/reduce_scatter | solution.py:170
  1048.4 20.7 %all-gather.4 = bf16[16,2,3456]{2,1,0:T(2,128)(2,1)S(1)} all-gather(bf16[1,2,3456]{2,1,0:T(2,128)(2,1)S(1)} %fusion.54), channel_id=1, replica_groups=mesh['dp'=16,'seq'=2] {'dp'}, dimensions={0}, use_global_device_ids=true | all-gather | bytes 235008 | tf_op jit(solution)/shard_map/all_gather | solution.py:299
  1071.5 8.0 add_bitcast_fusion
  1082.1 39.2 %all-reduce.4 = (f32[]{:T(128)}, f32[6912]{0:T(1024)}, f32[2304]{0:T(1024)}, f32[1152]{0:T(1024)}, f32[4608]{0:T(1024)}, /*index=5*/f32[1152]{0:T(1024)}) all-reduce(f32[]{:T(128)} %get-tuple-element.69, f32[6912]{0:T(1024)S(1)} %dynamic_update_slice.7, ...), channel_id=1, replica_groups=mesh['dp'=16,'seq'=2] {'dp','seq'}, use_global_device_ids=true, to_apply=%region_12.13 | all-reduce | flops 16129 | bytes 129032 | tf_op jit(solution)/shard_map/psum | solution.py:311
  1128.0 68.1 %all-reduce.8.cloned.1.call-done = f32[24,1152]{1,0:T(8,128)} async-done(((f32[24,1152]{1,0:T(8,128)}), f32[24,1152]{1,0:T(8,128)}) %all-reduce.8.cloned.1.call-update) | async-done | bytes 110608 | tf_op jit(solution)/shard_map/psum | solution.py:311
  (200 shorter events, 46.5 us)
Async XLA Ops:
  8.0 16.3 %copy-start.23 = (bf16[72,576]{1,0:T(8,128)(2,1)S(1)}, bf16[72,576]{1,0:T(8,128)(2,1)}, u32[]{:S(2)}) copy-start(bf16[72,576]{1,0:T(8,128)(2,1)} %param.26) | copy-start | bytes 248836
  8.0 97.2 %all-reduce.10.cloned.1.call-start = ((), (), s32[]{:S(2)}) async-start(), calls=%async_computation.22 | async-start | bytes 884736
  9.0 13.6 %copy-start.44 = (s32[32]{0:T(128)}, s32[32]{0:T(128)S(1)}, u32[]{:S(2)}) copy-start(s32[32]{0:T(128)S(1)} %eq.15) | copy-start | bytes 388
  11.9 98.9 %all-gather.19.cloned.1.call-start = ((), (), s32[]{:S(2)}) async-start(), calls=%async_computation.18 | async-start | bytes 7077888 | tf_op jit(solution)/shard_map/all_gather | solution.py:210
  12.5 157.7 %all-gather.11.cloned.1.call-start = ((), (), s32[]{:S(2)}) async-start(), calls=%async_computation.9 | async-start | bytes 8460288 | tf_op jit(solution)/shard_map/all_gather | solution.py:175
  23.0 52.7 %copy-start.43 = (s32[2,16]{1,0:T(2,128)S(1)}, s32[2,16]{1,0:T(2,128)}, u32[]{:S(2)}) copy-start(s32[2,16]{1,0:T(2,128)} %param.18) | copy-start | bytes 388
  23.0 54.3 %copy-start.48 = (u32[32]{0:T(128)S(1)}, u32[32]{0:T(128)}, u32[]{:S(2)}) copy-start(u32[32]{0:T(128)} %constant.77) | copy-start | bytes 388
  23.0 55.5 %copy-start.37 = (f32[2304]{0:T(1024)S(1)}, f32[2304]{0:T(1024)}, u32[]{:S(2)}) copy-start(f32[2304]{0:T(1024)} %param.25) | copy-start | bytes 27652
  23.1 55.5 %copy-start.12 = (bf16[2,1,512,1152]{3,2,1,0:T(8,128)(2,1)S(1)}, bf16[2,1,512,1152]{3,2,1,0:T(8,128)(2,1)}, u32[]{:S(2)}) copy-start(bf16[2,1,512,1152]{3,2,1,0:T(8,128)(2,1)} %param.21) | copy-start | bytes 7077892
  24.3 224.9 %all-gather.13.cloned.1.call-start = ((), (), s32[]{:S(2)}) async-start(), calls=%async_computation.10 | async-start | bytes 2820096 | tf_op jit(solution)/shard_map/all_gather | solution.py:175
  32.4 271.9 %all-gather.15.cloned.1.call-start = ((), (), s32[]{:S(2)}) async-start(), calls=%async_computation.11 | async-start | bytes 11280384 | tf_op jit(solution)/shard_map/all_gather | solution.py:175
  52.5 341.3 %all-gather.17.cloned.1.call-start = ((), (), s32[]{:S(2)}) async-start(), calls=%async_computation.12 | async-start | bytes 11280384 | tf_op jit(solution)/shard_map/all_gather | solution.py:175
  75.7 543.9 %reduce-scatter.36.cloned.1.call-start = ((), (), s32[]{:S(2)}) async-start(), calls=%async_computation.24 | async-start | bytes 2820096
  78.6 32.1 %copy-start.36 = (f32[6912]{0:T(1024)S(1)}, f32[6912]{0:T(1024)}, u32[]{:S(2)}) copy-start(f32[6912]{0:T(1024)} %param.23) | copy-start | bytes 82948
  120.6 56.3 %copy-start.18 = (bf16[2,512,1152]{2,1,0:T(8,128)(2,1)}, bf16[2,512,1152]{2,1,0:T(8,128)(2,1)S(1)}, u32[]{:S(2)}) copy-start(bf16[2,512,1152]{2,1,0:T(8,128)(2,1)S(1)} %constant_dynamic-slice_fusion.2) | copy-start | bytes 7077892
  170.2 6.7 copy-start.10
  170.2 6.7 copy-start.46
  191.2 58.0 %copy-start.47 = (f32[1152]{0:T(1024)S(1)}, f32[1152]{0:T(1024)}, u32[]{:S(2)}) copy-start(f32[1152]{0:T(1024)} %param.27) | copy-start | bytes 13828
  249.1 6.1 copy-start.2
  261.9 131.9 %copy-start.39 = (f32[4608]{0:T(1024)S(1)}, f32[4608]{0:T(1024)}, u32[]{:S(2)}) copy-start(f32[4608]{0:T(1024)} %param.29) | copy-start | bytes 55300
  261.9 131.9 %copy-start.40 = (f32[1152]{0:T(1024)S(1)}, f32[1152]{0:T(1024)}, u32[]{:S(2)}) copy-start(f32[1152]{0:T(1024)} %param.31) | copy-start | bytes 13828
  393.8 27.4 %copy-start.11 = (bf16[4608,1152]{1,0:T(8,128)(2,1)S(1)}, bf16[4608,1152]{1,0:T(8,128)(2,1)}, u32[]{:S(2)}) copy-start(bf16[4608,1152]{1,0:T(8,128)(2,1)} %all-gather.17.cloned.1.call-done) | copy-start | bytes 31850500
  469.3 8.2 copy-start.4
  469.3 8.7 copy-start.8
  469.3 9.4 copy-start.13
  469.3 10.1 copy-start.14
  469.3 10.0 copy-start.42
  490.7 6.7 copy-start.17
  497.4 208.3 %reduce-scatter.30.cloned.1.call-start = ((), (), s32[]{:S(2)}) async-start(), calls=%async_computation.20 | async-start | bytes 442368
  504.0 87.8 %copy-start.19 = (bf16[2,512,1152]{2,1,0:T(8,128)(2,1)S(1)}, bf16[2,512,1152]{2,1,0:T(8,128)(2,1)}, u32[]{:S(2)}) copy-start(bf16[2,512,1152]{2,1,0:T(8,128)(2,1)} %copy-done.18) | copy-start | bytes 7077892
  621.4 115.6 %reduce-scatter.34.cloned.1.call-start = ((), (), s32[]{:S(2)}) async-start(), calls=%async_computation.23 | async-start | bytes 8460288
  627.8 171.0 %reduce-scatter.20.cloned.1.call-start = ((), (), s32[]{:S(2)}) async-start(), calls=%async_computation.13 | async-start | bytes 7077888 | tf_op jit(solution)/shard_map/reduce_scatter | solution.py:287
  649.1 274.6 %reduce-scatter.26.cloned.1.call-start = ((), (), s32[]{:S(2)}) async-start(), calls=%async_computation.17 | async-start | bytes 11280384 | tf_op jit(solution)/shard_map/reduce_scatter | solution.py:170
  674.5 373.7 %reduce-scatter.22.cloned.1.call-start = ((), (), s32[]{:S(2)}) async-start(), calls=%async_computation.15 | async-start | bytes 11280384 | tf_op jit(solution)/shard_map/reduce_scatter | solution.py:170
  693.4 428.6 %reduce-scatter.28.cloned.1.call-start = ((), (), s32[]{:S(2)}) async-start(), calls=%async_computation.19 | async-start | bytes 1327104
  699.2 99.7 %copy-start.25 = (f32[2,1152]{1,0:T(2,128)S(1)}, f32[2,1152]{1,0:T(2,128)}, u32[]{:S(2)}) copy-start(f32[2,1152]{1,0:T(2,128)} %copy-done.24) | copy-start | bytes 27652
  739.3 384.7 %reduce-scatter.32.cloned.1.call-start = ((), (), s32[]{:S(2)}) async-start(), calls=%async_computation.21 | async-start | bytes 1327104
  798.8 127.2 %copy-start.33 = (f32[2,1152]{1,0:T(2,128)S(1)}, f32[2,1152]{1,0:T(2,128)}, u32[]{:S(2)}) copy-start(f32[2,1152]{1,0:T(2,128)} %get-tuple-element.93) | copy-start | bytes 27652
  798.8 127.2 %copy-start.32 = (f32[2,1152]{1,0:T(2,128)S(1)}, f32[2,1152]{1,0:T(2,128)}, u32[]{:S(2)}) copy-start(f32[2,1152]{1,0:T(2,128)} %get-tuple-element.74) | copy-start | bytes 27652
  798.8 127.3 %copy-start.31 = (f32[2,1152]{1,0:T(2,128)S(1)}, f32[2,1152]{1,0:T(2,128)}, u32[]{:S(2)}) copy-start(f32[2,1152]{1,0:T(2,128)} %get-tuple-element.73) | copy-start | bytes 27652
  798.9 127.3 %copy-start.30 = (f32[2,1152]{1,0:T(2,128)S(1)}, f32[2,1152]{1,0:T(2,128)}, u32[]{:S(2)}) copy-start(f32[2,1152]{1,0:T(2,128)} %get-tuple-element.68) | copy-start | bytes 27652
  809.4 259.9 %copy-start.45 = (s32[32]{0:T(128)S(1)}, s32[32]{0:T(128)}, u32[]{:S(2)}) copy-start(s32[32]{0:T(128)} %copy-done.44) | copy-start | bytes 388
  809.4 262.0 %copy-start.15 = (bf16[2,512,1152]{2,1,0:T(8,128)(2,1)S(1)}, bf16[2,512,1152]{2,1,0:T(8,128)(2,1)}, u32[]{:S(2)}) copy-start(bf16[2,512,1152]{2,1,0:T(8,128)(2,1)} %reduce-scatter.20.cloned.1.call-done) | copy-start | bytes 7077892
  926.0 200.2 %reduce-scatter.24.cloned.1.call-start = ((), (), s32[]{:S(2)}) async-start(), calls=%async_computation.16 | async-start | bytes 995328 | tf_op jit(solution)/shard_map/reduce_scatter | solution.py:171
  1048.3 147.8 %all-reduce.8.cloned.1.call-start = ((), (), s32[]{:S(2)}) async-start(), calls=%async_computation.14 | async-start | bytes 221184 | tf_op jit(solution)/shard_map/psum | solution.py:311
  1071.5 10.6 copy-start.34
  1071.5 10.6 copy-start.35
  1071.5 10.6 copy-start.38
  (17 other events, 42.7 us)
Sparse Core Ops, SparseCore 0:
  12.8 92.3 all-reduce.9
  497.5 62.0 reduce-scatter.35
  1071.6 124.4 all-reduce.7
Sparse Core Ops, SparseCore 1:
  13.9 81.2 all-gather.18
  97.8 72.3 all-gather.10
  172.8 42.0 all-gather.12
  217.2 87.1 all-gather.14
  307.2 86.5 all-gather.16
  621.5 10.0 reduce-scatter.29
  636.1 100.8 reduce-scatter.33
  739.2 59.6 reduce-scatter.19
  803.3 120.3 reduce-scatter.25
  928.3 119.9 reduce-scatter.21
  1050.5 18.1 reduce-scatter.27
  1071.0 18.7 reduce-scatter.31
  1091.9 16.3 reduce-scatter.23
